TPU v7x, 512 devices: a whole 4x4x16 slice. The times are simulated.
512 devices in a mesh: pair: 64 (over x, y, z_hi), sector: 8 (over z_lo, core).
Axes of the slice: x: 4, y: 4, z: 16 (z_hi: 4, z_lo: 4; z = z_hi * 4 + z_lo), core: 2. Of those that a mesh axis runs over, the one named last changes fastest.
Arguments:
- site_tensor: bfloat16 [4, 16, 128, 128], P(None, 'sector', 'pair'), may hold values from -0.5 to 0.5
- operators: bfloat16 [1536, 16, 128, 128], P('pair', 'sector'), may hold values from -6 to 6
- one_index: bfloat16 [128, 16, 128, 128], P('pair', 'sector'), may hold values from -6 to 6
- weights: bfloat16 [1536, 128], P('pair'), may hold values from -1 to 1
- comp_charge: int32 [1536], P('pair'), may hold values from 0 to 2
- one_charge: int32 [128], replicated, may hold values from 0 to 2
- sector_size: int32 [16], replicated, may hold values from 1 to 128, 1280 in all
- coupling: int32 [16, 4], replicated, may hold values from 0 to 16, as said below
Outputs:
- renormalized: bfloat16 [1536, 16, 128, 128], P('pair', 'sector')
Inputs may be any that keep to these rules, and one draw needn't show every extreme that they name: coupling[s, t] = min(s + c[t], 16) where c is an arrangement of the charges 0, 1, 1, 2 over the 4 orbital states; the value 16 marks a dropped combination.
All inputs are finite; a program needn't handle non-finite values.
Results may differ from a plain program's by a relative error of at most 0.007.
Values may be sent and summed in bfloat16 or wider, within the bound.
No kernel may reach another device: no remote copies, remote signals or barrier semaphores. Data moves between devices by JAX's collectives and lax.ppermute only.
A program may use at most 64 MiB of HBM per device.

v0:
```python
import jax
import jax.numpy as jnp
from jax import lax
from jax.sharding import PartitionSpec as P


def from_behind(value, axis, steps):
    count = lax.axis_size(axis)
    initial, last = (max(0, -steps), min(count, count - steps))
    return lax.ppermute(value, axis, [(source, source + steps) for source in range(initial, last)])


def body(
    site_tensor, operators, one_index, weights, comp_charge, one_charge, sector_size, coupling
):
    sec_local = operators.shape[1]
    block_size = operators.shape[2]
    ops_local = operators.shape[0]
    states = site_tensor.shape[0]
    total_sectors = sec_local * lax.axis_size("sector")
    first_sector = lax.axis_index("sector") * sec_local
    full_site = lax.all_gather(site_tensor, "pair", axis=2, tiled=True)
    positions = jnp.arange(block_size, dtype=jnp.int32)
    own_sizes = lax.dynamic_slice_in_dim(sector_size, first_sector, sec_local)
    live_rows = positions[None, :] < own_sizes[:, None]
    own_site = jnp.where(live_rows[None, :, :, None], full_site, jnp.zeros((), jnp.bfloat16))
    upper_blocks = from_behind(own_site, "sector", -1)
    right_pool = jnp.concatenate([own_site, upper_blocks], axis=1)
    matching = comp_charge[:, None] == one_charge[None, :]
    coef = jnp.where(matching, weights, jnp.zeros((), jnp.bfloat16))
    shard_piece = lax.all_gather(one_index, "pair", axis=0, tiled=True)
    piece_rows = shard_piece.shape[0]
    flattened = shard_piece.reshape(piece_rows, -1)
    summed = jnp.dot(coef, flattened, preferred_element_type=jnp.float32)
    combined = (operators.astype(jnp.float32) + summed.reshape(operators.shape)).astype(
        jnp.bfloat16
    )
    state_charge = coupling[0]
    pool_count = right_pool.shape[1]
    global_right = (
        first_sector + jnp.arange(sec_local, dtype=jnp.int32)[None, :] + comp_charge[:, None]
    )
    in_range = global_right < total_sectors
    pool_index = jnp.clip(global_right - first_sector, 0, pool_count - 1)
    gathered_out = jnp.zeros((ops_local, sec_local + 2, block_size, block_size), jnp.float32)
    for local_state in range(states):
        right_blocks = right_pool[local_state][pool_index]
        right_blocks = jnp.where(
            in_range[:, :, None, None], right_blocks, jnp.zeros((), jnp.bfloat16)
        )
        partial_value = jnp.einsum(
            "ksij,ksjc->ksic", combined, right_blocks, preferred_element_type=jnp.float32
        ).astype(jnp.bfloat16)
        contrib = jnp.einsum(
            "sia,ksic->ksac",
            own_site[local_state],
            partial_value,
            preferred_element_type=jnp.float32,
        )
        offset = state_charge[local_state]
        current = lax.dynamic_slice_in_dim(gathered_out, offset, sec_local, 1)
        gathered_out = lax.dynamic_update_slice_in_dim(gathered_out, current + contrib, offset, 1)
    carried = from_behind(gathered_out[:, sec_local:].astype(jnp.bfloat16), "sector", 1).astype(
        jnp.float32
    )
    landed = gathered_out[:, :sec_local].at[:, :2].add(carried)
    return landed.astype(jnp.bfloat16)


def solution(mesh):
    return jax.shard_map(
        body,
        mesh=mesh,
        in_specs=(
            P(None, "sector", "pair", None),
            P("pair", "sector", None, None),
            P("pair", "sector", None, None),
            P("pair", None),
            P("pair"),
            P(),
            P(),
            P(),
        ),
        out_specs=P("pair", "sector", None, None),
        check_vma=False,
    )
```

profile of v0, /device:TPU:38, one launch (start us, length us, event | category | flops | bytes accessed | tf_op | source)
XLA Modules:
  0.0 383.1 jit_solution(11426421221952369991)
XLA Ops:
  6.5 0.7 all-gather.2.cloned.1.call-update
  7.3 0.7 copy.17
  8.0 0.7 dynamic_slice.12
  8.7 249.5 %all_gather.7 = bf16[4,2,128,128]{3,0,1,2:T(4,128)(2,1)S(1)} all-gather(bf16[4,2,2,128]{3,0,1,2:T(4,128)(2,1)S(1)} %copy.17), channel_id=1, replica_groups=mesh['pair'=64,'sector'=8] {'pair'}, dimensions={2}, use_global_device_ids=true | all-gather | bytes 266240 | tf_op jit(solution)/shard_map/all_gather | solution.py:22
  258.2 0.1 iota_compare_fusion
  258.3 0.1 copy_select_fusion.16
  258.4 1.9 collective-permute-start
  260.3 0.7 compare_select_fusion
  261.1 0.1 reshape.165
  261.2 1.4 fusion.49
  270.1 0.7 add_compare_fusion
  270.9 0.0 collective-permute-done
  270.9 1.9 gather_fusion
  272.9 1.9 gather_fusion.1
  274.8 2.0 gather_fusion.2
  276.8 0.8 gather_fusion.3
  277.6 0.0 copy-start
  277.6 0.0 copy-start.1
  277.6 0.0 copy-start.2
  277.7 0.0 all-gather.2.cloned.1.call-done
  277.7 12.7 %copy.41 = bf16[128,2,128,128]{0,3,2,1:T(8,128)(2,1)} copy(bf16[128,2,128,128]{3,2,1,0:T(8,128)(2,1)} %all-gather.2.cloned.1.call-done) | data formatting | bytes 16777216 | tf_op jit(solution)/shard_map/reshape | solution.py:33
  290.4 8.3 %add_convert_fusion = bf16[24,2,128,128]{3,0,2,1:T(8,128)(2,1)S(1)} fusion(bf16[128,2,128,128]{0,3,2,1:T(8,128)(2,1)} %copy.41, bf16[24,2,128,128]{3,2,1,0:T(8,128)(2,1)} %param.13, bf16[24,128]{1,0:T(8,128)(2,1)S(1)} %copy-done, s32[128]{0:T(128)S(1)} %copy-done.2, s32[24]{0:T(128)S(1)} %copy-done.1), kind=kOutput, calls=%fused_computation.16 | convolution fusion | flops 203692032 | bytes 11541088 | tf_op jit(solution)/shard_map/dot_general | solution.py:34
  298.7 3.5 broadcast_in_dim.58
  302.1 4.1 %bitcast_dynamic-update-slice_fusion = f32[24,4,128,128]{2,3,0,1:T(8,128)} fusion(f32[24,4,128,128]{2,3,0,1:T(8,128)} %broadcast_in_dim.58, s32[]{:T(128)S(6)} %select_n.57, bf16[24,2,128,128]{3,2,1,0:T(8,128)(2,1)} %bitcast.73, pred[24,2]{0,1:T(4,128)(4,1)S(1)} %add_compare_fusion, bf16[24,2,128,128]{3,0,2,1:T(8,128)(2,1)S(1)} %add_convert_fusion, ...), kind=kOutput, calls=%fused_computation.15 | convolution fusion | flops 404226048 | bytes 6357508 | tf_op jit(solution)/shard_map/sia,ksic->ksac/dot_general | solution.py:54
  306.2 5.1 %fusion.5 = f32[24,4,128,128]{2,3,0,1:T(8,128)} fusion(f32[24,4,128,128]{2,3,0,1:T(8,128)} %bitcast_dynamic-update-slice_fusion, s32[]{:T(128)S(6)} %select_n.58, bf16[24,2,128,128]{3,2,1,0:T(8,128)(2,1)} %bitcast.72, pred[24,2]{0,1:T(4,128)(4,1)S(1)} %add_compare_fusion, bf16[24,2,128,128]{3,0,2,1:T(8,128)(2,1)S(1)} %add_convert_fusion, ...), kind=kOutput, calls=%fused_computation.14 | convolution fusion | flops 405012480 | bytes 9503236 | tf_op jit(solution)/shard_map/sia,ksic->ksac/dot_general | solution.py:54
  311.3 5.1 %fusion.4 = f32[24,4,128,128]{2,3,0,1:T(8,128)} fusion(f32[24,4,128,128]{2,3,0,1:T(8,128)} %fusion.5, s32[]{:T(128)S(6)} %select_n.60, bf16[24,2,128,128]{3,2,1,0:T(8,128)(2,1)} %bitcast.71, pred[24,2]{0,1:T(4,128)(4,1)S(1)} %add_compare_fusion, bf16[24,2,128,128]{3,0,2,1:T(8,128)(2,1)S(1)} %add_convert_fusion, ...), kind=kOutput, calls=%fused_computation.12 | convolution fusion | flops 405012480 | bytes 9503236 | tf_op jit(solution)/shard_map/sia,ksic->ksac/dot_general | solution.py:54
  316.3 4.6 %fusion.3 = f32[24,4,128,128]{2,3,0,1:T(8,128)} fusion(f32[24,4,128,128]{2,3,0,1:T(8,128)} %fusion.4, s32[]{:T(128)S(6)} %select_n.62, bf16[24,2,128,128]{3,2,1,0:T(8,128)(2,1)S(1)} %bitcast.70, pred[24,2]{0,1:T(4,128)(4,1)S(1)} %add_compare_fusion, bf16[24,2,128,128]{3,0,2,1:T(8,128)(2,1)S(1)} %add_convert_fusion, ...), kind=kOutput, calls=%fused_computation.10 | convolution fusion | flops 405012480 | bytes 9503236 | tf_op jit(solution)/shard_map/sia,ksic->ksac/dot_general | solution.py:54
  321.0 2.1 slice.146
  323.1 2.4 collective-permute-start.1
  325.5 46.7 %collective-permute-done.1 = bf16[24,2,128,128]{2,3,0,1:T(8,128)(2,1)S(1)} collective-permute-done((bf16[24,2,128,128]{2,3,0,1:T(8,128)(2,1)S(1)}, bf16[24,2,128,128]{2,3,0,1:T(8,128)(2,1)S(1)}, u32[]{:S(2)}, u32[]{:S(2)}) %collective-permute-start.1) | collective-permute-done | bytes 1572896 | tf_op jit(solution)/shard_map/ppermute | solution.py:10
  372.3 2.4 fusion.2
  374.7 1.6 copy.31
  (7 shorter events, 0.1 us)
Async XLA Ops:
  6.5 271.1 %all-gather.2.cloned.1.call-start = ((), (), s32[]{:S(2)}) async-start(), calls=%async_computation | async-start | bytes 8519680 | tf_op jit(solution)/shard_map/all_gather | solution.py:31
  258.4 12.5 %collective-permute-start = (bf16[4,2,128,128]{3,2,1,0:T(8,128)(2,1)S(1)}, bf16[4,2,128,128]{3,2,1,0:T(8,128)(2,1)S(1)}, u32[]{:S(2)}, u32[]{:S(2)}) collective-permute-start(bf16[4,2,128,128]{3,2,1,0:T(8,128)(2,1)S(1)} %copy_select_fusion.16), channel_id=1, source_target_pairs={{1,0},{2,1},{3,2},{4,3},{5,4},{6,5},{7,6},{9,8},{10,9},{11,10},{12... | collective-permute-start | bytes 786440 | tf_op jit(solution)/shard_map/ppermute | solution.py:10
  277.6 12.8 %copy-start = (bf16[24,128]{1,0:T(8,128)(2,1)S(1)}, bf16[24,128]{1,0:T(8,128)(2,1)}, u32[]{:S(2)}) copy-start(bf16[24,128]{1,0:T(8,128)(2,1)} %param.15) | copy-start | bytes 18436
  277.6 12.7 %copy-start.1 = (s32[24]{0:T(128)S(1)}, s32[24]{0:T(128)}, u32[]{:S(2)}) copy-start(s32[24]{0:T(128)} %param.16) | copy-start | bytes 292
  277.6 12.7 %copy-start.2 = (s32[128]{0:T(128)S(1)}, s32[128]{0:T(128)}, u32[]{:S(2)}) copy-start(s32[128]{0:T(128)} %param.17) | copy-start | bytes 1540
  323.1 49.1 %collective-permute-start.1 = (bf16[24,2,128,128]{2,3,0,1:T(8,128)(2,1)S(1)}, bf16[24,2,128,128]{2,3,0,1:T(8,128)(2,1)S(1)}, u32[]{:S(2)}, u32[]{:S(2)}) collective-permute-start(bf16[24,2,128,128]{2,3,0,1:T(8,128)(2,1)S(1)} %slice.146), channel_id=1, source_target_pairs={{0,1},{1,2},{2,3},{3,4},{4,5},{5,6},{6,7},{8,9},{9,10},{10,11},{11... | collective-permute-start | bytes 4718600 | tf_op jit(solution)/shard_map/ppermute | solution.py:10
Sparse Core Ops, SparseCore 0:
  11.5 168.6 all-gather.1
where the time goes:
time: 384 us; the launch traced here: 383 us
  blocking collectives  250 us (65%)
  waiting for transfers between devices  47.5 us (12%)
  local copies, waits for them, and re-layouts  29.5 us (8%)
  matrix products  27.1 us (7%)
  between operations  21.1 us (5%)
  starting transfers between devices  4.33 us (1%)
  other arithmetic  4.1 us (1%)
    all_gather x1, blocking collectives, body(): full_site = lax.all_gather(site_tensor, 'pair', axis=2, tiled=True)  250 us
    ppermute x2, waiting for transfers between devices, from_behind(): lax.ppermute(value, axis, [(source, source + steps) for source in range(i...  46.7 us
    dot_general x4, matrix products, body(): jnp.einsum('sia,ksic->ksac', own_site[local_state], partial_value, prefer...  18.9 us
    reshape x1, local copies, waits for them, and re-layouts, body(): flattened = shard_piece.reshape(piece_rows, -1)  12.7 us
    dot_general x1, matrix products, body(): summed = jnp.dot(coef, flattened, preferred_element_type=jnp.float32)  8.28 us
  transfers between devices with their start and end apart: 3, of which 1 were waited for; matrix products, arithmetic and copies ran while one was open for 3% of the time, Pallas kernels for 0%

commit v1 on v0

--- a/solution.py
+++ b/solution.py
@@ -2,6 +2,11 @@
 import jax.numpy as jnp
 from jax import lax
 from jax.sharding import PartitionSpec as P
+
+
+def swapped_in(x, name, dim):
+    sent = jnp.stack([x] * lax.axis_size(name))
+    return jnp.concatenate(lax.all_to_all(sent, name, 0, 0), axis=dim)
 
 
 def from_behind(value, axis, steps):
@@ -19,7 +24,7 @@
     states = site_tensor.shape[0]
     total_sectors = sec_local * lax.axis_size("sector")
     first_sector = lax.axis_index("sector") * sec_local
-    full_site = lax.all_gather(site_tensor, "pair", axis=2, tiled=True)
+    full_site = swapped_in(site_tensor, "pair", 2)
     positions = jnp.arange(block_size, dtype=jnp.int32)
     own_sizes = lax.dynamic_slice_in_dim(sector_size, first_sector, sec_local)
     live_rows = positions[None, :] < own_sizes[:, None]

time: 384 us -> 291 us (0.76)
  the two profiles are of different devices: /device:TPU:38 before, /device:TPU:1 now
where the time goes in v1:
time: 291 us; the launch traced here: 290 us
  waiting for transfers between devices  177 us (61%)
  starting transfers between devices  31.1 us (11%)
  local copies, waits for them, and re-layouts  30.5 us (10%)
  matrix products  27.1 us (9%)
  between operations  20.8 us (7%)
  other arithmetic  3.44 us (1%)
    all_gather x1, waiting for transfers between devices, body(): shard_piece = lax.all_gather(one_index, 'pair', axis=0, tiled=True)  140 us
    all_to_all x1, starting transfers between devices, swapped_in(): return jnp.concatenate(lax.all_to_all(sent, name, 0, 0), axis=dim)  21.7 us
    ppermute x2, waiting for transfers between devices, from_behind(): lax.ppermute(value, axis, [(source, source + steps) for source in range(i...  21 us
    dot_general x4, matrix products, body(): jnp.einsum('sia,ksic->ksac', own_site[local_state], partial_value, prefer...  18.8 us
    all_to_all x1, waiting for transfers between devices, swapped_in(): return jnp.concatenate(lax.all_to_all(sent, name, 0, 0), axis=dim)  15.1 us
    reshape x1, local copies, waits for them, and re-layouts, body(): flattened = shard_piece.reshape(piece_rows, -1)  12.6 us
    ppermute x2, starting transfers between devices, from_behind(): lax.ppermute(value, axis, [(source, source + steps) for source in range(i...  9.41 us
    dot_general x1, matrix products, body(): summed = jnp.dot(coef, flattened, preferred_element_type=jnp.float32)  8.28 us
  transfers between devices with their start and end apart: 4, of which 4 were waited for; matrix products, arithmetic and copies ran while one was open for 4% of the time, Pallas kernels for 0%

profile of v1, /device:TPU:1, one launch (start us, length us, event | category | flops | bytes accessed | tf_op | source)
XLA Modules:
  0.0 289.9 jit_solution(11286528494248785750)
XLA Ops:
  6.5 0.7 all-gather.2.cloned.1.call-update
  7.3 1.5 stack.2
  8.8 21.7 %all-to-all-start = ((bf16[64,4,2,2,128]{4,3,2,1,0:T(2,128)(2,1)}), bf16[64,4,2,2,128]{4,3,2,1,0:T(2,128)(2,1)S(1)}, u32[]{:S(2)}, u32[]{:S(2)}) async-start(bf16[64,4,2,2,128]{4,3,2,1,0:T(2,128)(2,1)} %stack.2), calls=%async_computation | async-start | bytes 524288 | tf_op jit(solution)/shard_map/all_to_all | solution.py:9
  30.5 0.7 compare_select_fusion
  31.3 0.1 reshape.175
  31.4 0.7 dynamic_slice.12
  32.1 1.4 fusion.49
  33.5 0.1 iota_compare_fusion
  33.6 15.1 %all-to-all-done = bf16[64,4,2,2,128]{4,3,2,1,0:T(2,128)(2,1)S(1)} async-done(((bf16[64,4,2,2,128]{4,3,2,1,0:T(2,128)(2,1)}), bf16[64,4,2,2,128]{4,3,2,1,0:T(2,128)(2,1)S(1)}, u32[]{:S(2)}, u32[]{:S(2)}) %all-to-all-start) | async-done | bytes 262176 | tf_op jit(solution)/shard_map/all_to_all | solution.py:9
  48.7 0.2 copy.17
  48.9 0.1 broadcast_select_fusion
  49.0 7.5 %collective-permute-start = (bf16[4,2,128,128]{3,2,1,0:T(8,128)(2,1)S(1)}, bf16[4,2,128,128]{3,2,1,0:T(8,128)(2,1)S(1)}, u32[]{:S(2)}, u32[]{:S(2)}) collective-permute-start(bf16[4,2,128,128]{3,2,1,0:T(8,128)(2,1)S(1)} %broadcast_select_fusion), channel_id=1, source_target_pairs={{1,0},{2,1},{3,2},{4,3},{5,4},{6,5},{7,6},{9,8},{10,9},{11,10},{12... | collective-permute-start | bytes 786440 | tf_op jit(solution)/shard_map/ppermute | solution.py:15
  63.8 0.1 add_compare_fusion
  63.9 3.7 %collective-permute-done = bf16[4,2,128,128]{3,2,1,0:T(8,128)(2,1)S(1)} collective-permute-done((bf16[4,2,128,128]{3,2,1,0:T(8,128)(2,1)S(1)}, bf16[4,2,128,128]{3,2,1,0:T(8,128)(2,1)S(1)}, u32[]{:S(2)}, u32[]{:S(2)}) %collective-permute-start) | collective-permute-done | bytes 262176 | tf_op jit(solution)/shard_map/ppermute | solution.py:15
  67.6 1.9 gather_fusion
  69.5 2.0 gather_fusion.1
  71.5 2.0 gather_fusion.2
  73.5 0.8 gather_fusion.3
  74.3 0.0 copy-start
  74.3 140.2 %all-gather.2.cloned.1.call-done = bf16[128,2,128,128]{3,2,1,0:T(8,128)(2,1)} async-done(((bf16[2,2,128,128]{3,2,1,0:T(8,128)(2,1)}), bf16[128,2,128,128]{3,2,1,0:T(8,128)(2,1)}) %all-gather.2.cloned.1.call-update) | async-done | bytes 8388624 | tf_op jit(solution)/shard_map/all_gather | solution.py:36
  214.5 12.6 %copy.40 = bf16[128,2,128,128]{0,3,2,1:T(8,128)(2,1)} copy(bf16[128,2,128,128]{3,2,1,0:T(8,128)(2,1)} %all-gather.2.cloned.1.call-done) | data formatting | bytes 16777216 | tf_op jit(solution)/shard_map/reshape | solution.py:38
  227.1 8.3 %add_convert_fusion = bf16[24,2,128,128]{3,0,2,1:T(8,128)(2,1)S(1)} fusion(bf16[128,2,128,128]{0,3,2,1:T(8,128)(2,1)} %copy.40, bf16[24,2,128,128]{3,2,1,0:T(8,128)(2,1)} %param.13, bf16[24,128]{1,0:T(8,128)(2,1)S(1)} %copy-done, s32[128]{0:T(128)S(1)} %copy-done.2, s32[24]{0:T(128)S(1)} %copy-done.1), kind=kOutput, calls=%fused_computation.16 | convolution fusion | flops 203692032 | bytes 11541088 | tf_op jit(solution)/shard_map/dot_general | solution.py:39
  235.4 3.4 %broadcast_in_dim.58 = f32[24,4,128,128]{2,3,0,1:T(8,128)} broadcast(f32[]{:T(128)} %constant.48.clone.1), dimensions={} | broadcast | bytes 6291460 | tf_op jit(solution)/shard_map/broadcast_in_dim | solution.py:50
  238.9 4.1 %bitcast_dynamic-update-slice_fusion = f32[24,4,128,128]{2,3,0,1:T(8,128)} fusion(f32[24,4,128,128]{2,3,0,1:T(8,128)} %broadcast_in_dim.58, s32[]{:T(128)S(6)} %select_n.57, bf16[24,2,128,128]{3,2,1,0:T(8,128)(2,1)} %bitcast.75, pred[24,2]{0,1:T(4,128)(4,1)S(1)} %add_compare_fusion, bf16[24,2,128,128]{3,0,2,1:T(8,128)(2,1)S(1)} %add_convert_fusion, ...), kind=kOutput, calls=%fused_computation.15 | convolution fusion | flops 404226048 | bytes 6357508 | tf_op jit(solution)/shard_map/sia,ksic->ksac/dot_general | solution.py:59
  242.9 5.1 %fusion.5 = f32[24,4,128,128]{2,3,0,1:T(8,128)} fusion(f32[24,4,128,128]{2,3,0,1:T(8,128)} %bitcast_dynamic-update-slice_fusion, s32[]{:T(128)S(6)} %select_n.58, bf16[24,2,128,128]{3,2,1,0:T(8,128)(2,1)} %bitcast.74, pred[24,2]{0,1:T(4,128)(4,1)S(1)} %add_compare_fusion, bf16[24,2,128,128]{3,0,2,1:T(8,128)(2,1)S(1)} %add_convert_fusion, ...), kind=kOutput, calls=%fused_computation.14 | convolution fusion | flops 405012480 | bytes 9503236 | tf_op jit(solution)/shard_map/sia,ksic->ksac/dot_general | solution.py:59
  248.0 5.0 %fusion.4 = f32[24,4,128,128]{2,3,0,1:T(8,128)} fusion(f32[24,4,128,128]{2,3,0,1:T(8,128)} %fusion.5, s32[]{:T(128)S(6)} %select_n.60, bf16[24,2,128,128]{3,2,1,0:T(8,128)(2,1)} %bitcast.73, pred[24,2]{0,1:T(4,128)(4,1)S(1)} %add_compare_fusion, bf16[24,2,128,128]{3,0,2,1:T(8,128)(2,1)S(1)} %add_convert_fusion, ...), kind=kOutput, calls=%fused_computation.12 | convolution fusion | flops 405012480 | bytes 9503236 | tf_op jit(solution)/shard_map/sia,ksic->ksac/dot_general | solution.py:59
  253.1 4.6 %fusion.3 = f32[24,4,128,128]{2,3,0,1:T(8,128)} fusion(f32[24,4,128,128]{2,3,0,1:T(8,128)} %fusion.4, s32[]{:T(128)S(6)} %select_n.62, bf16[24,2,128,128]{3,2,1,0:T(8,128)(2,1)S(1)} %bitcast.72, pred[24,2]{0,1:T(4,128)(4,1)S(1)} %add_compare_fusion, bf16[24,2,128,128]{3,0,2,1:T(8,128)(2,1)S(1)} %add_convert_fusion, ...), kind=kOutput, calls=%fused_computation.10 | convolution fusion | flops 405012480 | bytes 9503236 | tf_op jit(solution)/shard_map/sia,ksic->ksac/dot_general | solution.py:59
  257.7 2.1 slice.146
  259.8 1.9 collective-permute-start.1
  261.8 17.3 %collective-permute-done.1 = bf16[24,2,128,128]{2,3,0,1:T(8,128)(2,1)S(1)} collective-permute-done((bf16[24,2,128,128]{2,3,0,1:T(8,128)(2,1)S(1)}, bf16[24,2,128,128]{2,3,0,1:T(8,128)(2,1)S(1)}, u32[]{:S(2)}, u32[]{:S(2)}) %collective-permute-start.1) | collective-permute-done | bytes 1572896 | tf_op jit(solution)/shard_map/ppermute | solution.py:15
  279.1 2.4 fusion.2
  281.5 1.6 copy.30
  (9 shorter events, 0.1 us)
Async XLA Ops:
  6.5 57.2 %copy-start.1 = (s32[24]{0:T(128)S(1)}, s32[24]{0:T(128)}, u32[]{:S(2)}) copy-start(s32[24]{0:T(128)} %param.16) | copy-start | bytes 292
  6.5 207.9 %all-gather.2.cloned.1.call-start = ((), (), s32[]{:S(2)}) async-start(), calls=%async_computation.1 | async-start | bytes 8519680 | tf_op jit(solution)/shard_map/all_gather | solution.py:36
  8.8 39.9 %all-to-all-start = ((bf16[64,4,2,2,128]{4,3,2,1,0:T(2,128)(2,1)}), bf16[64,4,2,2,128]{4,3,2,1,0:T(2,128)(2,1)S(1)}, u32[]{:S(2)}, u32[]{:S(2)}) async-start(bf16[64,4,2,2,128]{4,3,2,1,0:T(2,128)(2,1)} %stack.2), calls=%async_computation | async-start | bytes 524288 | tf_op jit(solution)/shard_map/all_to_all | solution.py:9
  49.0 18.6 %collective-permute-start = (bf16[4,2,128,128]{3,2,1,0:T(8,128)(2,1)S(1)}, bf16[4,2,128,128]{3,2,1,0:T(8,128)(2,1)S(1)}, u32[]{:S(2)}, u32[]{:S(2)}) collective-permute-start(bf16[4,2,128,128]{3,2,1,0:T(8,128)(2,1)S(1)} %broadcast_select_fusion), channel_id=1, source_target_pairs={{1,0},{2,1},{3,2},{4,3},{5,4},{6,5},{7,6},{9,8},{10,9},{11,10},{12... | collective-permute-start | bytes 786440 | tf_op jit(solution)/shard_map/ppermute | solution.py:15
  74.3 152.8 %copy-start = (bf16[24,128]{1,0:T(8,128)(2,1)S(1)}, bf16[24,128]{1,0:T(8,128)(2,1)}, u32[]{:S(2)}) copy-start(bf16[24,128]{1,0:T(8,128)(2,1)} %param.15) | copy-start | bytes 18436
  74.3 152.8 %copy-start.2 = (s32[128]{0:T(128)S(1)}, s32[128]{0:T(128)}, u32[]{:S(2)}) copy-start(s32[128]{0:T(128)} %param.17) | copy-start | bytes 1540
  259.8 19.3 %collective-permute-start.1 = (bf16[24,2,128,128]{2,3,0,1:T(8,128)(2,1)S(1)}, bf16[24,2,128,128]{2,3,0,1:T(8,128)(2,1)S(1)}, u32[]{:S(2)}, u32[]{:S(2)}) collective-permute-start(bf16[24,2,128,128]{2,3,0,1:T(8,128)(2,1)S(1)} %slice.146), channel_id=1, source_target_pairs={{0,1},{1,2},{2,3},{3,4},{4,5},{5,6},{6,7},{8,9},{9,10},{10,11},{11... | collective-permute-start | bytes 4718600 | tf_op jit(solution)/shard_map/ppermute | solution.py:15
Sparse Core Ops, SparseCore 0:
  11.5 202.9 all-gather.1
